TPU v7x, 32 devices: a whole 2x2x4 slice. The times are simulated.
32 devices in a mesh: groups: 2 (over x), mix: 16 (over z, y, core).
Axes of the slice: x: 2, y: 2, z: 4, core: 2. Of those that a mesh axis runs over, the one named last changes fastest.
Arguments:
- resid_in: bfloat16 [4096, 2048], P(('groups', 'mix')), parts along dimension 0, may hold values from -40 to 40
- head_in: bfloat16 [4096, 4096], P('groups', 'mix'), parts along dimension 0, may hold values from -6 to 6
- gate_in: bfloat16 [4096, 4096], P('groups', 'mix'), parts along dimension 0, may hold values from -64 to 64
- in_basis: bfloat16 [4096, 128], P('groups'), parts along dimension 0, may hold values from -6 to 6
- out_basis: bfloat16 [4096, 128], P('groups'), parts along dimension 0, may hold values from -6 to 6
- step_size: float32 [64, 4096], P('mix', 'groups'), parts along dimension 1, may hold values from 0 to 2
- decay_rate: float32 [64], P('mix'), may hold values from 0.5 to 2
- init_state: float32 [16, 64, 64, 128], P('groups', 'mix'), parts along dimension 0, may hold values from -0.6 to 0.6
- lengths: int32 [16], P('groups'), parts along dimension 0, may hold values from 1 to 512, 2048 in all
- norm_gain: float32 [4096], replicated, may hold values from 0.1 to 1.9
- out_proj: bfloat16 [4096, 2048], P('mix'), may hold values from -0.09375 to 0.09375
- moe_gain: float32 [2048], replicated, may hold values from 0.1 to 1.9
- expert_ids: int32 [4096, 8], P(('groups', 'mix')), parts along dimension 0, may hold values from 0 to 31, as said below
- route_weight: float32 [4096, 8], P(('groups', 'mix')), parts along dimension 0, may hold values from 0.1 to 0.4
- placement: int32 [32], replicated, may hold values from 0 to 31, each once
- w_gate: bfloat16 [32, 2048, 768], P('mix'), may hold values from -0.125 to 0.125
- w_up: bfloat16 [32, 2048, 768], P('mix'), may hold values from -0.125 to 0.125
- w_down: bfloat16 [32, 768, 2048], P('mix'), may hold values from -0.21875 to 0.21875
Outputs:
- layer_out: bfloat16 [4096, 2048], P(('groups', 'mix')), parts along dimension 0
There are 2 independent parts, one for each index of `groups`. A program takes and returns all parts, laid end to end along the dimension named above; an argument that names none is the same for every part. Nothing has to cross between parts.
Inputs may be any that keep to these rules, and one draw needn't show every extreme that they name: `expert_ids`: each row names 8 different experts. Within each aligned block of 128 rows (one device's rows), 8 experts appear exactly 64 times each, 8 others 64 / 2 times each and the rest 64 / 4 times each; each of the three sets is the same in every block. `placement`: each slot once. `lengths`: requests fill the 2048 positions in order.
All inputs are finite; a program needn't handle non-finite values.
Results may differ from a plain program's by a relative error of at most 0.013.
Values may be sent and summed in bfloat16 or wider, within the bound.
No kernel may reach another device: no remote copies, remote signals or barrier semaphores. Data moves between devices by JAX's collectives and lax.ppermute only.
A program may use at most 128 MiB of HBM per device.

v0:
```python
import jax
import jax.numpy as jnp
from jax import lax
from jax.sharding import PartitionSpec as P

HEADS = 64
HEAD_DIM = 64
SPAN = 256
epsilon = 1e-05


def request_layout(lengths, tokens_total):
    request_end = jnp.cumsum(lengths)
    request_first = request_end - lengths
    position = jnp.arange(tokens_total, dtype=jnp.int32)
    segment = jnp.sum((position[None, :] >= request_end[:, None]).astype(jnp.int32), axis=0)
    member = segment[None, :] == jnp.arange(lengths.shape[0], dtype=jnp.int32)[:, None]
    first_of = jnp.sum(jnp.where(member, request_first[:, None], 0), axis=0)
    return (segment, first_of, member)


def scan_heads(
    head_values,
    head_steps,
    head_rates,
    in_basis,
    out_basis,
    state_init,
    segment,
    first_of,
    member,
    block_len,
):
    tokens_total = head_values.shape[0]
    local_heads = head_steps.shape[0]
    head_width = head_values.shape[1] // local_heads
    blocks = tokens_total // block_len
    highest = lax.Precision.HIGHEST
    log_decay = -head_steps * head_rates[:, None]
    driven = (
        head_values.reshape(tokens_total, local_heads, head_width)
        .transpose(1, 0, 2)
        .astype(jnp.float32)
    )
    driven = driven * head_steps[:, :, None]
    drive_split = driven.reshape(local_heads, blocks, block_len, head_width).transpose(1, 0, 2, 3)
    decay_split = log_decay.reshape(local_heads, blocks, block_len).transpose(1, 0, 2)

    def split_rows(array):
        return array.reshape((blocks, block_len) + array.shape[1:])

    block_first = jnp.arange(blocks, dtype=jnp.int32) * block_len
    member_blocks = member.reshape(member.shape[0], blocks, block_len).transpose(1, 0, 2)
    init_heads = state_init.transpose(1, 0, 2, 3)
    inputs = (
        drive_split,
        decay_split,
        split_rows(in_basis),
        split_rows(out_basis),
        split_rows(segment),
        split_rows(first_of),
        member_blocks,
        block_first,
    )
    offsets = jnp.arange(block_len, dtype=jnp.int32)
    causal = offsets[None, :] <= offsets[:, None]

    def advance(states_in, block_in):
        (
            drive_heads,
            decay_heads,
            basis_block,
            readout_block,
            segment_block,
            first_block,
            member_block,
            first_pos,
        ) = block_in
        basis_wide = basis_block.astype(jnp.float32)
        readout_wide = readout_block.astype(jnp.float32)
        same_seq = (segment_block[:, None] == segment_block[None, :]) & causal
        scores = jnp.dot(readout_block, basis_block.T, preferred_element_type=jnp.float32)
        carried = first_block < first_pos
        member_wide = member_block.astype(jnp.float32)

        def one_head(state_in, drive_block, decay_block, head_init):
            running = jnp.cumsum(decay_block)
            earlier = running - decay_block
            gap_values = jnp.minimum(running[:, None] - running[None, :], 0.0)
            kernel = jnp.where(same_seq, jnp.exp(gap_values), 0.0)
            output = jnp.dot(kernel * scores, drive_block, precision=highest)
            before = jnp.max(jnp.where(same_seq, earlier[None, :], -jnp.inf), axis=1)
            weight = jnp.exp(running - before)
            from_state = jnp.dot(readout_wide, state_in.T, precision=highest)
            projected = jnp.einsum("qn,rpn->rqp", readout_wide, head_init, precision=highest)
            from_init = jnp.sum(member_wide[:, :, None] * projected, axis=0)
            output = output + weight[:, None] * jnp.where(carried[:, None], from_state, from_init)
            last_weight = jnp.where(same_seq[-1], jnp.exp(running[-1] - running), 0.0)
            state_out = jnp.dot(
                (drive_block * last_weight[:, None]).T, basis_wide, precision=highest
            )
            init_last = jnp.einsum("r,rpn->pn", member_wide[:, -1], head_init, precision=highest)
            source = jnp.where(carried[-1], state_in, init_last)
            state_out = state_out + weight[-1] * source
            return (state_out, output)

        return jax.vmap(one_head)(states_in, drive_heads, decay_heads, init_heads)

    empty_state = jnp.zeros((local_heads, head_width, in_basis.shape[1]), jnp.float32)
    _, outputs = lax.scan(advance, empty_state, inputs)
    return outputs.transpose(0, 2, 1, 3).reshape(tokens_total, local_heads * head_width)


def local(
    resid_in,
    head_in,
    gate_in,
    in_basis,
    out_basis,
    step_size,
    decay_rate,
    init_state,
    lengths,
    norm_gain,
    out_proj,
    moe_gain,
    expert_ids,
    route_weight,
    placement,
    w_gate,
    w_up,
    w_down,
):
    tokens_total = head_in.shape[0]
    model_width = out_proj.shape[1]
    devices = lax.axis_size("mix")
    tok_rows = tokens_total // devices
    segment, first_of, member = request_layout(lengths, tokens_total)
    scan_out = scan_heads(
        head_in,
        step_size,
        decay_rate,
        in_basis,
        out_basis,
        init_state,
        segment,
        first_of,
        member,
        SPAN,
    )
    gated_out = scan_out * jax.nn.silu(gate_in.astype(jnp.float32))
    regrouped = lax.all_to_all(
        gated_out.astype(jnp.bfloat16), "mix", split_axis=0, concat_axis=1, tiled=True
    ).astype(gated_out.dtype)
    squares = jnp.sum(regrouped * regrouped, axis=1)
    mixed_in = (regrouped * norm_gain).astype(jnp.bfloat16)
    full_proj = lax.all_gather(out_proj, "mix", axis=0, tiled=True)
    group_terms = jnp.einsum(
        "tgc,gcd->tgd",
        mixed_in.reshape(tok_rows, devices, -1),
        full_proj.reshape(devices, -1, model_width),
        preferred_element_type=jnp.float32,
    ).astype(jnp.bfloat16)
    group_terms = lax.optimization_barrier(group_terms)
    mixer_sum = jnp.sum(group_terms.astype(jnp.float32), axis=1)
    mixer_out = mixer_sum * lax.rsqrt(squares / (HEADS * HEAD_DIM) + epsilon)[:, None]
    hidden = resid_in.astype(jnp.float32) + mixer_out
    normed = (
        hidden * lax.rsqrt(jnp.mean(hidden * hidden, axis=1, keepdims=True) + epsilon) * moe_gain
    ).astype(jnp.bfloat16)
    top_count = expert_ids.shape[1]
    flat_ids = expert_ids.reshape(-1)
    pair_count = flat_ids.shape[0]
    experts_total = placement.shape[0]
    cap_slots = 2 * pair_count // experts_total
    choose = (flat_ids[:, None] == jnp.arange(experts_total, dtype=jnp.int32)[None, :]).astype(
        jnp.int32
    )
    slot_of = jnp.sum(choose * placement[None, :], axis=1)
    slot_rank = jnp.sum(jnp.cumsum(choose, axis=0) * choose, axis=1) - 1
    buffer_index = slot_of * cap_slots + slot_rank
    owner_token = (
        jnp.full((experts_total * cap_slots,), -1, jnp.int32)
        .at[buffer_index]
        .set(jnp.arange(pair_count, dtype=jnp.int32) // top_count)
    )
    filled = owner_token >= 0
    send_rows = jnp.where(
        filled[:, None],
        jnp.take(normed, jnp.maximum(owner_token, 0), axis=0),
        jnp.zeros((), jnp.bfloat16),
    )
    send_rows = send_rows.reshape(devices, experts_total // devices, cap_slots, model_width)
    received = lax.all_to_all(send_rows, "mix", split_axis=0, concat_axis=0, tiled=True)
    gate_part = jnp.einsum("sekd,edf->sekf", received, w_gate, preferred_element_type=jnp.float32)
    up_part = jnp.einsum("sekd,edf->sekf", received, w_up, preferred_element_type=jnp.float32)
    inner_act = (jax.nn.silu(gate_part) * up_part).astype(jnp.bfloat16)
    result = jnp.einsum(
        "sekf,efd->sekd", inner_act, w_down, preferred_element_type=jnp.float32
    ).astype(jnp.bfloat16)
    returned_rows = lax.all_to_all(result, "mix", split_axis=0, concat_axis=0, tiled=True)
    back_flat = returned_rows.reshape(experts_total * cap_slots, model_width)
    picked = jnp.take(back_flat, buffer_index, axis=0).reshape(tok_rows, top_count, model_width)
    expert_sum = jnp.sum(route_weight[:, :, None] * picked.astype(jnp.float32), axis=1)
    return (hidden + expert_sum).astype(jnp.bfloat16)


def solution(mesh):
    return jax.shard_map(
        local,
        mesh=mesh,
        in_specs=(
            P(("groups", "mix"), None),
            P("groups", "mix"),
            P("groups", "mix"),
            P("groups", None),
            P("groups", None),
            P("mix", "groups"),
            P("mix"),
            P("groups", "mix", None, None),
            P("groups"),
            P(),
            P("mix", None),
            P(),
            P(("groups", "mix"), None),
            P(("groups", "mix"), None),
            P(),
            P("mix", None, None),
            P("mix", None, None),
            P("mix", None, None),
        ),
        out_specs=P(("groups", "mix"), None),
        check_vma=False,
    )
```

profile of v0, /device:TPU:15, one launch (start us, length us, event | category | flops | bytes accessed | tf_op | source)
XLA Modules:
  0.0 655.7 jit_solution(5398734231998708079)
XLA Ops:
  11.5 2.2 copy.110
  15.5 123.0 %while.13 = (s32[]{:T(128)}, f32[4,64,128]{2,1,0:T(8,128)S(1)}, f32[8,4,256,64]{2,3,1,0:T(8,128)}, f32[8,4,256,64]{2,0,3,1:T(8,128)}, s32[8,256]{1,0:T(8,128)S(1...) while((s32[]{:T(128)}, f32[4,64,128]{2,1,0:T(8,128)S(1)}, ...), condition=%wide.region_8.9_spmd.clone, body=%wide.region_3.8_spmd.clone.sunk | while | flops 1231164672 | bytes 6564249 | solution.py:110
  17.8 1.9 fusion.115
  23.2 1.8 constant_dynamic-slice_fusion.7
  25.0 2.2 fusion.116
  33.2 1.9 fusion.115
  38.6 1.8 constant_dynamic-slice_fusion.7
  40.4 2.1 fusion.116
  44.5 1.7 convolution_add_fusion.3
  48.6 1.9 fusion.115
  54.0 1.8 constant_dynamic-slice_fusion.7
  55.8 2.2 fusion.116
  64.0 1.9 fusion.115
  69.4 1.8 constant_dynamic-slice_fusion.7
  71.2 2.2 fusion.116
  75.3 1.7 convolution_add_fusion.3
  79.4 1.9 fusion.115
  84.8 1.8 constant_dynamic-slice_fusion.7
  86.6 2.2 fusion.116
  94.8 1.9 fusion.115
  100.1 1.8 constant_dynamic-slice_fusion.7
  101.9 2.1 fusion.116
  110.2 1.9 fusion.115
  115.5 1.8 constant_dynamic-slice_fusion.7
  117.3 2.1 fusion.116
  121.4 1.7 convolution_add_fusion.3
  125.5 1.9 fusion.115
  130.9 1.8 constant_dynamic-slice_fusion.7
  132.6 2.2 fusion.116
  138.5 2.9 copy.89
  143.8 1.9 fusion.62
  147.0 6.7 %all-to-all-start = ((bf16[16,128,256]{2,1,0:T(8,128)(2,1)}), bf16[16,128,256]{2,1,0:T(8,128)(2,1)S(1)}, u32[]{:S(2)}, u32[]{:S(2)}) async-start(bf16[16,128,256]{2,1,0:T(8,128)(2,1)} %bitcast.11), calls=%async_computation | async-start | bytes 2097152 | tf_op jit(solution)/shard_map/all_to_all | solution.py:152
  154.1 9.0 %reduce-window.26 = s32[32,8,128]{2,1,0:T(8,128)S(1)} reduce-window(s32[32,8,128]{2,1,0:T(8,128)S(1)} %fusion.68, s32[]{:T(128)} %constant.97.clone.1), window={size=1x1x128 pad=0_0x0_0x127_0}, to_apply=%region_12.13 | reduce-window | flops 4161536 | bytes 262148 | tf_op jit(solution)/shard_map/reduce-window.3
  163.7 4.3 scatter_custom_fusion
  168.2 10.4 %all-to-all-done = bf16[16,128,256]{2,1,0:T(8,128)(2,1)S(1)} async-done(((bf16[16,128,256]{2,1,0:T(8,128)(2,1)}), bf16[16,128,256]{2,1,0:T(8,128)(2,1)S(1)}, u32[]{:S(2)}, u32[]{:S(2)}) %all-to-all-start) | async-done | bytes 1048608 | tf_op jit(solution)/shard_map/all_to_all | solution.py:152
  178.9 11.4 %convert_bitcast_fusion.1 = bf16[128,16,2048]{2,0,1:T(8,128)(2,1)} fusion(bf16[16,256,2048]{2,1,0:T(8,128)(2,1)} %bitcast.224, bf16[16,128,256]{2,1,0:T(8,128)(2,1)S(1)} %all-to-all-done, f32[16,256]{1,0:T(8,128)S(1)} %mul.163), kind=kOutput, calls=%fused_computation.66 | convolution fusion | flops 2153250816 | bytes 26230784 | tf_op jit(solution)/shard_map/tgc,gcd->tgd/dot_general | solution.py:158
  190.3 5.3 convert_reduce_fusion
  196.3 11.0 %gather_fusion = bf16[2048,2048]{1,0:T(8,128)(2,1)} fusion(bf16[128,2048]{1,0:T(8,128)(2,1)S(1)} %multiply_convert_fusion, s32[2048]{0:T(1024)S(1)} %maximum_clamp_fusion), kind=kCustom, calls=%fused_computation | custom fusion | bytes 16785408 | tf_op jit(solution)/shard_map/jit(_take)/gather | solution.py:190
  207.3 4.6 select_select_fusion
  212.0 187.0 %all_to_all.23 = bf16[16,2,64,2048]{3,2,1,0:T(8,128)(2,1)S(1)} all-to-all(bf16[16,2,64,2048]{3,2,1,0:T(8,128)(2,1)S(1)} %select_select_fusion), channel_id=1, replica_groups=mesh['groups'=2,'mix'=16] {'mix'}, dimensions={0} | all-to-all | bytes 16777216 | tf_op jit(solution)/shard_map/all_to_all | solution.py:194
  398.9 10.6 %fusion.39 = f32[2,16,64,768]{3,2,1,0:T(8,128)} fusion(bf16[16,2,64,2048]{3,2,1,0:T(8,128)(2,1)S(1)} %all_to_all.23, bf16[2,2048,768]{2,1,0:T(8,128)(2,1)} %param.36), kind=kOutput, calls=%fused_computation.67 | convolution fusion | flops 6442450944 | bytes 20971520 | tf_op jit(solution)/shard_map/sekd,edf->sekf/dot_general | solution.py:196
  409.6 8.5 %fusion.41 = f32[2,16,64,768]{3,2,1,0:T(8,128)} fusion(bf16[16,2,64,2048]{3,2,1,0:T(8,128)(2,1)S(1)} %all_to_all.23, bf16[2,2048,768]{2,1,0:T(8,128)(2,1)S(1)} %bitcast.249), kind=kOutput, calls=%fused_computation.69 | convolution fusion | flops 6442450944 | bytes 20971520 | tf_op jit(solution)/shard_map/sekd,edf->sekf/dot_general | solution.py:195
  418.1 14.5 %convert_bitcast_fusion = bf16[16,2,64,2048]{3,2,0,1:T(8,128)(2,1)} fusion(bf16[2,768,2048]{2,1,0:T(8,128)(2,1)} %param.37, f32[2,16,64,768]{3,2,1,0:T(8,128)} %fusion.39, f32[2,16,64,768]{3,2,1,0:T(8,128)} %fusion.41), kind=kOutput, calls=%fused_computation.64 | convolution fusion | flops 6456082432 | bytes 27262976 | tf_op jit(solution)/shard_map/sekf,efd->sekd/dot_general | solution.py:198
  432.6 8.3 %copy.99 = bf16[16,2,64,2048]{3,2,1,0:T(8,128)(2,1)} copy(bf16[16,2,64,2048]{3,2,0,1:T(8,128)(2,1)} %convert_bitcast_fusion) | data formatting | bytes 16777216 | tf_op jit(solution)/shard_map/convert_element_type | solution.py:200
  440.8 5.7 all-to-all-start.2
  446.8 182.1 %all-to-all-done.2 = bf16[16,2,64,2048]{3,2,1,0:T(8,128)(2,1)} async-done(((bf16[16,2,64,2048]{3,2,1,0:T(8,128)(2,1)}), bf16[16,2,64,2048]{3,2,1,0:T(8,128)(2,1)}, u32[]{:S(2)}, u32[]{:S(2)}) %all-to-all-start.2) | async-done | bytes 8388640 | tf_op jit(solution)/shard_map/all_to_all | solution.py:201
  628.9 13.3 %gather_fusion.1 = bf16[1024,2048]{1,0:T(8,128)(2,1)} fusion(bf16[2048,2048]{1,0:T(8,128)(2,1)} %bitcast.29, s32[1024]{0:T(1024)S(1)} %broadcast_clamp_fusion), kind=kCustom, calls=%fused_computation.1 | custom fusion | bytes 8392704 | tf_op jit(solution)/shard_map/jit(_take)/gather | solution.py:203
  642.2 5.6 multiply_reduce_fusion
  (293 shorter events, 84.1 us)
Async XLA Ops:
  6.5 8.8 %copy-start.2 = (f32[4,2048]{1,0:T(4,128)S(1)}, f32[4,2048]{1,0:T(4,128)}, u32[]{:S(2)}) copy-start(f32[4,2048]{1,0:T(4,128)} %param.25) | copy-start | bytes 98308
  6.5 8.9 %copy-start.7 = (f32[4]{0:T(128)S(1)}, f32[4]{0:T(128)}, u32[]{:S(2)}) copy-start(f32[4]{0:T(128)} %param.26) | copy-start | bytes 52
  6.5 172.4 %all-gather.2.cloned.1.call-start = ((), (), s32[]{:S(2)}) async-start(), calls=%async_computation.3 | async-start | bytes 17825792 | tf_op jit(solution)/shard_map/all_gather | solution.py:157
  138.5 3.8 copy-start.1
  142.3 11.4 %copy-start.5 = (s32[128,8]{0,1:T(8,128)S(1)}, s32[128,8]{0,1:T(8,128)}, u32[]{:S(2)}) copy-start(s32[128,8]{0,1:T(8,128)} %param.32) | copy-start | bytes 12292
  142.3 11.7 %copy-start.3 = (f32[4096]{0:T(1024)S(1)}, f32[4096]{0:T(1024)}, u32[]{:S(2)}) copy-start(f32[4096]{0:T(1024)} %param.29) | copy-start | bytes 49156
  142.3 21.2 %copy-start.8 = (s32[32]{0:T(128)S(1)}, s32[32]{0:T(128)}, u32[]{:S(2)}) copy-start(s32[32]{0:T(128)} %param.34) | copy-start | bytes 388
  147.0 31.6 %all-to-all-start = ((bf16[16,128,256]{2,1,0:T(8,128)(2,1)}), bf16[16,128,256]{2,1,0:T(8,128)(2,1)S(1)}, u32[]{:S(2)}, u32[]{:S(2)}) async-start(bf16[16,128,256]{2,1,0:T(8,128)(2,1)} %bitcast.11), calls=%async_computation | async-start | bytes 2097152 | tf_op jit(solution)/shard_map/all_to_all | solution.py:152
  190.3 5.4 copy-start
  190.3 5.7 copy-start.4
  211.9 197.6 %slice-start = ((s8[6291456]{0:T(1024)(128)(4,1)}), s8[4194304]{0:T(1024)(128)(4,1)S(1)}, s32[]{:S(2)}) async-start(s8[6291456]{0:T(1024)(128)(4,1)} %bitcast.248), calls=%async_computation.4 | async-start | bytes 8388608
  398.9 10.6 %slice-start.1 = ((s8[6291456]{0:T(1024)(128)(4,1)}), s8[2097152]{0:T(1024)(128)(4,1)S(1)}, s32[]{:S(2)}) async-start(s8[6291456]{0:T(1024)(128)(4,1)} %bitcast.248), calls=%async_computation.5 | async-start | bytes 4194304
  440.8 5.8 copy-start.6
  440.8 188.1 %all-to-all-start.2 = ((bf16[16,2,64,2048]{3,2,1,0:T(8,128)(2,1)}), bf16[16,2,64,2048]{3,2,1,0:T(8,128)(2,1)}, u32[]{:S(2)}, u32[]{:S(2)}) async-start(bf16[16,2,64,2048]{3,2,1,0:T(8,128)(2,1)} %copy.99), calls=%async_computation.2 | async-start | bytes 16777216 | tf_op jit(solution)/shard_map/all_to_all | solution.py:201
Sparse Core Ops, SparseCore 0:
  9.5 125.3 all-gather.1
where the time goes:
time: 658 us; the launch traced here: 656 us
  waiting for transfers between devices  193 us (29%)
  blocking collectives  187 us (28%)
  matrix products  118 us (18%)
  local copies, waits for them, and re-layouts  79.6 us (12%)
  other arithmetic  51.1 us (8%)
  between operations  13.8 us (2%)
  starting transfers between devices  12.5 us (2%)
    all_to_all x1, blocking collectives, local(): lax.all_to_all(send_rows, 'mix', split_axis=0, concat_axis=0, tiled=True)  187 us
    all_to_all x1, waiting for transfers between devices, local(): lax.all_to_all(result, 'mix', split_axis=0, concat_axis=0, tiled=True)  182 us
    another operation x20, other arithmetic  20.1 us
    dynamic_slice x32, local copies, waits for them, and re-layouts, scan_heads(): _, outputs = lax.scan(advance, empty_state, inputs)  19.4 us
    dot_general x8, matrix products, one_head(): output = jnp.dot(kernel * scores, drive_block, precision=highest)  17.2 us
    dot_general x8, matrix products, one_head(): jnp.einsum('qn,rpn->rqp', readout_wide, head_init, precision=highest)  14.9 us
    dot_general x1, matrix products, local(): jnp.einsum('sekf,efd->sekd', inner_act, w_down, preferred_element_type=jn...  14.5 us
    dot_general x8, matrix products, one_head(): jnp.dot((drive_block * last_weight[:, None]).T, basis_wide, precision=hig...  13.8 us
  transfers between devices with their start and end apart: 3, of which 2 were waited for; matrix products, arithmetic and copies ran while one was open for 23% of the time, Pallas kernels for 0%

commit v1 on v0

--- a/solution.py
+++ b/solution.py
@@ -7,6 +7,18 @@
 HEAD_DIM = 64
 SPAN = 256
 epsilon = 1e-05
+
+
+def in_blocks(shard, dim, size):
+    shape = shard.shape
+    blocks = shard.reshape(*shape[:dim], size, shape[dim] // size, *shape[dim + 1 :])
+    return jnp.moveaxis(blocks, dim, 0)
+
+
+def laid_out(blocks, dim):
+    dims = list(blocks.shape[1:])
+    dims[dim] *= blocks.shape[0]
+    return jnp.moveaxis(blocks, 0, dim).reshape(dims)
 
 
 def request_layout(lengths, tokens_total):
@@ -198,7 +210,15 @@
     result = jnp.einsum(
         "sekf,efd->sekd", inner_act, w_down, preferred_element_type=jnp.float32
     ).astype(jnp.bfloat16)
-    returned_rows = lax.all_to_all(result, "mix", split_axis=0, concat_axis=0, tiled=True)
+    size, index = (lax.axis_size("mix"), lax.axis_index("mix"))
+    pieces = in_blocks(result, 0, size)
+    out = pieces
+    for step in range(1, size):
+        target, source_2 = ((index + step) % size, (index - step) % size)
+        sent = lax.dynamic_index_in_dim(pieces, target, 0)
+        theirs = lax.ppermute(sent, "mix", [(i, (i + step) % size) for i in range(size)])
+        out = lax.dynamic_update_slice_in_dim(out, theirs, source_2, axis=0)
+    returned_rows = laid_out(out, 0)
     back_flat = returned_rows.reshape(experts_total * cap_slots, model_width)
     picked = jnp.take(back_flat, buffer_index, axis=0).reshape(tok_rows, top_count, model_width)
     expert_sum = jnp.sum(route_weight[:, :, None] * picked.astype(jnp.float32), axis=1)

time: 658 us -> 688 us (1.046)
  blocking collectives: 187 us -> 0 us
  waiting for transfers between devices: 193 us -> 369 us
  local copies, waits for them, and re-layouts: 79.6 us -> 102 us
    all_to_all x1 -> x0, blocking collectives: 187 us -> none  [local(): lax.all_to_all(send_rows, 'mix', split_axis=0, concat_axis=0, tiled=True)]
    ppermute x0 -> x15, waiting for transfers between devices: none -> 176 us  [local(): lax.ppermute(sent, 'mix', [(i, (i + step) % size) for i in range(size)])]
    dynamic_update_slice x0 -> x16, local copies, waits for them, and re-layouts: none -> 23.7 us  [local(): out = lax.dynamic_update_slice_in_dim(out, theirs, source_2, axis=0)]
    convert_element_type x1 -> x0, local copies, waits for them, and re-layouts: 8.25 us -> none  [local(): result = jnp.einsum('sekf,efd->sekd', inner_act, w_down, preferred_elemen...]
    ppermute x0 -> x15, starting transfers between devices: none -> 6.9 us  [local(): lax.ppermute(sent, 'mix', [(i, (i + step) % size) for i in range(size)])]
  transfers between devices with their start and end apart: 3 -> 18, of which waited for: 2 -> 12; matrix products, arithmetic and copies ran while one was open for 23% -> 25% of each run, Pallas kernels for 0% -> 0%
where the time goes in v1:
time: 688 us; the launch traced here: 683 us
  waiting for transfers between devices  369 us (54%)
  matrix products  124 us (18%)
  local copies, waits for them, and re-layouts  102 us (15%)
  other arithmetic  53.9 us (8%)
  starting transfers between devices  18.3 us (3%)
  between operations  14.3 us (2%)
    all_to_all x1, waiting for transfers between devices, local(): lax.all_to_all(send_rows, 'mix', split_axis=0, concat_axis=0, tiled=True)  182 us
    ppermute x15, waiting for transfers between devices, local(): lax.ppermute(sent, 'mix', [(i, (i + step) % size) for i in range(size)])  176 us
    dynamic_update_slice x16, local copies, waits for them, and re-layouts, local(): out = lax.dynamic_update_slice_in_dim(out, theirs, source_2, axis=0)  23.7 us
    dynamic_slice x32, local copies, waits for them, and re-layouts, scan_heads(): _, outputs = lax.scan(advance, empty_state, inputs)  20.5 us
    another operation x20, other arithmetic  20.1 us
    dot_general x8, matrix products, one_head(): output = jnp.dot(kernel * scores, drive_block, precision=highest)  17.2 us
    dot_general x8, matrix products, one_head(): jnp.einsum('qn,rpn->rqp', readout_wide, head_init, precision=highest)  14.9 us
    dot_general x1, matrix products, local(): jnp.einsum('sekf,efd->sekd', inner_act, w_down, preferred_element_type=jn...  14.5 us
  transfers between devices with their start and end apart: 18, of which 12 were waited for; matrix products, arithmetic and copies ran while one was open for 25% of the time, Pallas kernels for 0%

profile of v1, /device:TPU:15, one launch (start us, length us, event | category | flops | bytes accessed | tf_op | source)
XLA Modules:
  0.0 682.7 jit_solution(8164375477084490839)
XLA Ops:
  11.4 2.2 copy.110
  15.5 124.0 %while.13 = (s32[]{:T(128)}, f32[4,64,128]{2,1,0:T(8,128)S(1)}, f32[8,4,256,64]{2,3,1,0:T(8,128)}, f32[8,4,256,64]{2,0,3,1:T(8,128)}, s32[8,256]{1,0:T(8,128)S(1...) while((s32[]{:T(128)}, f32[4,64,128]{2,1,0:T(8,128)S(1)}, ...), condition=%wide.region_8.9_spmd.clone, body=%wide.region_3.8_spmd.clone.sunk | while | flops 1231164672 | bytes 6562225 | solution.py:122
  28.7 2.2 fusion.117
  42.2 1.9 fusion.116
  44.1 2.1 fusion.117
  59.4 2.2 fusion.117
  61.6 2.4 constant_dynamic-slice_fusion.7
  73.5 1.9 fusion.116
  75.4 2.2 fusion.117
  90.7 2.2 fusion.117
  104.2 1.9 fusion.116
  106.1 2.1 fusion.117
  108.2 2.3 constant_dynamic-slice_fusion.7
  122.0 2.1 fusion.117
  137.3 2.2 fusion.117
  139.5 2.9 copy.89
  144.7 1.9 fusion.63
  147.9 6.5 all-to-all-start
  154.8 9.0 %reduce-window.26 = s32[32,8,128]{2,1,0:T(8,128)S(1)} reduce-window(s32[32,8,128]{2,1,0:T(8,128)S(1)} %fusion.69, s32[]{:T(128)} %constant.287.clone.1), window={size=1x1x128 pad=0_0x0_0x127_0}, to_apply=%region_12.13 | reduce-window | flops 4161536 | bytes 262148 | tf_op jit(solution)/shard_map/reduce-window.3
  164.4 4.3 scatter_custom_fusion
  168.9 10.4 %all-to-all-done = bf16[16,128,256]{2,1,0:T(8,128)(2,1)S(1)} async-done(((bf16[16,128,256]{2,1,0:T(8,128)(2,1)}), bf16[16,128,256]{2,1,0:T(8,128)(2,1)S(1)}, u32[]{:S(2)}, u32[]{:S(2)}) %all-to-all-start) | async-done | bytes 1048608 | tf_op jit(solution)/shard_map/all_to_all | solution.py:164
  179.7 11.4 %convert_bitcast_fusion = bf16[128,16,2048]{2,0,1:T(8,128)(2,1)} fusion(bf16[16,256,2048]{2,1,0:T(8,128)(2,1)} %bitcast.256, bf16[16,128,256]{2,1,0:T(8,128)(2,1)S(1)} %all-to-all-done, f32[16,256]{1,0:T(8,128)S(1)} %mul.163), kind=kOutput, calls=%fused_computation.65 | convolution fusion | flops 2153250816 | bytes 26230784 | tf_op jit(solution)/shard_map/tgc,gcd->tgd/dot_general | solution.py:170
  191.0 5.3 convert_reduce_fusion
  197.1 11.0 %gather_fusion = bf16[2048,2048]{1,0:T(8,128)(2,1)} fusion(bf16[128,2048]{1,0:T(8,128)(2,1)S(1)} %multiply_convert_fusion, s32[2048]{0:T(1024)S(1)} %maximum_clamp_fusion), kind=kCustom, calls=%fused_computation | custom fusion | bytes 16785408 | tf_op jit(solution)/shard_map/jit(_take)/gather | solution.py:202
  208.1 7.4 %select_select_fusion = bf16[16,2,64,2048]{3,2,1,0:T(8,128)(2,1)} fusion(bf16[16,2,64,2048]{3,2,1,0:T(8,128)(2,1)} %bitcast.257, pred[16,2,64]{2,1,0:T(4,128)(4,1)S(1)} %broadcast_in_dim.137, pred[16,2,64]{2,1,0:T(4,128)(4,1)S(1)} %broadcast_in_dim.135), kind=kLoop, calls=%fused_computation.64 | loop fusion | flops 8388608 | bytes 16781312 | tf_op jit(solution)/shard_map/jit(_where)/select_n | solution.py:200
  215.4 4.9 all-to-all-start.1
  220.5 182.1 %all-to-all-done.1 = bf16[16,2,64,2048]{3,2,1,0:T(8,128)(2,1)} async-done(((bf16[16,2,64,2048]{3,2,1,0:T(8,128)(2,1)}), bf16[16,2,64,2048]{3,2,1,0:T(8,128)(2,1)}, u32[]{:S(2)}, u32[]{:S(2)}) %all-to-all-start.1) | async-done | bytes 8388640 | tf_op jit(solution)/shard_map/all_to_all | solution.py:206
  402.6 12.7 %fusion.39 = f32[2,16,64,768]{3,2,1,0:T(8,128)} fusion(bf16[16,2,64,2048]{3,2,1,0:T(8,128)(2,1)} %all-to-all-done.1, bf16[2,2048,768]{2,1,0:T(8,128)(2,1)} %param.36), kind=kOutput, calls=%fused_computation.66 | convolution fusion | flops 6442450944 | bytes 20971520 | tf_op jit(solution)/shard_map/sekd,edf->sekf/dot_general | solution.py:208
  415.3 12.6 %fusion.41 = f32[2,16,64,768]{3,2,1,0:T(8,128)} fusion(bf16[16,2,64,2048]{3,2,1,0:T(8,128)(2,1)} %all-to-all-done.1, bf16[2,2048,768]{2,1,0:T(8,128)(2,1)} %param.35), kind=kOutput, calls=%fused_computation.68 | convolution fusion | flops 6442450944 | bytes 20971520 | tf_op jit(solution)/shard_map/sekd,edf->sekf/dot_general | solution.py:207
  427.9 14.5 %fusion.51 = bf16[2,16,64,2048]{3,2,1,0:T(8,128)(2,1)} fusion(bf16[2,768,2048]{2,1,0:T(8,128)(2,1)} %param.37, f32[2,16,64,768]{3,2,1,0:T(8,128)} %fusion.39, f32[2,16,64,768]{3,2,1,0:T(8,128)} %fusion.41), kind=kOutput, calls=%fused_computation.81 | convolution fusion | flops 6456082432 | bytes 27262976 | tf_op jit(solution)/shard_map/sekf,efd->sekd/dot_general | solution.py:210
  442.4 6.0 dynamic-slice_bitcast_fusion.1
  451.8 3.6 collective-permute-start.4
  455.4 6.1 collective-permute-done
  461.7 1.9 constant_dynamic-update-slice_fusion.13
  463.6 9.3 %collective-permute-done.1 = bf16[1,1,2,64,2048]{4,3,0,2,1:T(8,128)(2,1)} collective-permute-done((bf16[1,1,2,64,2048]{4,3,0,2,1:T(8,128)(2,1)}, bf16[1,1,2,64,2048]{4,3,0,2,1:T(8,128)(2,1)}, u32[]{:S(2)}, u32[]{:S(2)}) %collective-permute-start.1) | collective-permute-done | bytes 524320 | tf_op jit(solution)/shard_map/ppermute | solution.py:219
  472.8 1.9 constant_dynamic-update-slice_fusion.12
  474.7 9.2 %collective-permute-done.2 = bf16[1,1,2,64,2048]{4,3,0,2,1:T(8,128)(2,1)} collective-permute-done((bf16[1,1,2,64,2048]{4,3,0,2,1:T(8,128)(2,1)}, bf16[1,1,2,64,2048]{4,3,0,2,1:T(8,128)(2,1)}, u32[]{:S(2)}, u32[]{:S(2)}) %collective-permute-start.2) | collective-permute-done | bytes 524320 | tf_op jit(solution)/shard_map/ppermute | solution.py:219
  483.9 1.9 constant_dynamic-update-slice_fusion.11
  485.8 59.9 %collective-permute-done.3 = bf16[1,1,2,64,2048]{4,3,0,2,1:T(8,128)(2,1)S(1)} collective-permute-done((bf16[1,1,2,64,2048]{4,3,0,2,1:T(8,128)(2,1)}, bf16[1,1,2,64,2048]{4,3,0,2,1:T(8,128)(2,1)S(1)}, u32[]{:S(2)}, u32[]{:S(2)}) %collective-permute-start.3) | collective-permute-done | bytes 524320 | tf_op jit(solution)/shard_map/ppermute | solution.py:219
  546.5 27.2 %collective-permute-done.4 = bf16[1,1,2,64,2048]{4,3,0,2,1:T(8,128)(2,1)S(1)} collective-permute-done((bf16[1,1,2,64,2048]{4,3,0,2,1:T(8,128)(2,1)}, bf16[1,1,2,64,2048]{4,3,0,2,1:T(8,128)(2,1)S(1)}, u32[]{:S(2)}, u32[]{:S(2)}) %collective-permute-start.4) | collective-permute-done | bytes 524320 | tf_op jit(solution)/shard_map/ppermute | solution.py:219
  574.6 16.0 %collective-permute-done.5 = bf16[1,1,2,64,2048]{4,3,0,2,1:T(8,128)(2,1)S(1)} collective-permute-done((bf16[1,1,2,64,2048]{4,3,0,2,1:T(8,128)(2,1)}, bf16[1,1,2,64,2048]{4,3,0,2,1:T(8,128)(2,1)S(1)}, u32[]{:S(2)}, u32[]{:S(2)}) %collective-permute-start.5) | collective-permute-done | bytes 524320 | tf_op jit(solution)/shard_map/ppermute | solution.py:219
  591.5 16.0 %collective-permute-done.6 = bf16[1,1,2,64,2048]{4,3,0,2,1:T(8,128)(2,1)S(1)} collective-permute-done((bf16[1,1,2,64,2048]{4,3,0,2,1:T(8,128)(2,1)}, bf16[1,1,2,64,2048]{4,3,0,2,1:T(8,128)(2,1)S(1)}, u32[]{:S(2)}, u32[]{:S(2)}) %collective-permute-start.6) | collective-permute-done | bytes 524320 | tf_op jit(solution)/shard_map/ppermute | solution.py:219
  608.3 16.0 %collective-permute-done.7 = bf16[1,1,2,64,2048]{4,3,0,2,1:T(8,128)(2,1)S(1)} collective-permute-done((bf16[1,1,2,64,2048]{4,3,0,2,1:T(8,128)(2,1)}, bf16[1,1,2,64,2048]{4,3,0,2,1:T(8,128)(2,1)S(1)}, u32[]{:S(2)}, u32[]{:S(2)}) %collective-permute-start.7) | collective-permute-done | bytes 524320 | tf_op jit(solution)/shard_map/ppermute | solution.py:219
  628.7 6.0 collective-permute-done.12
  635.6 10.4 %collective-permute-done.13 = bf16[1,1,2,64,2048]{4,3,0,2,1:T(8,128)(2,1)S(1)} collective-permute-done((bf16[1,1,2,64,2048]{4,3,0,2,1:T(8,128)(2,1)S(1)}, bf16[1,1,2,64,2048]{4,3,0,2,1:T(8,128)(2,1)S(1)}, u32[]{:S(2)}, u32[]{:S(2)}) %collective-permute-start.13) | collective-permute-done | bytes 524320 | tf_op jit(solution)/shard_map/ppermute | solution.py:219
  647.7 8.3 %copy.99 = bf16[16,1,2,64,2048]{4,3,2,0,1:T(8,128)(2,1)} copy(bf16[16,1,2,64,2048]{4,3,0,2,1:T(8,128)(2,1)} %constant_dynamic-update-slice_fusion.14) | data formatting | bytes 16777216 | tf_op jit(solution)/shard_map/dynamic_update_slice | solution.py:220
  655.9 13.3 %gather_fusion.1 = bf16[1024,2048]{1,0:T(8,128)(2,1)} fusion(bf16[2048,2048]{1,0:T(8,128)(2,1)} %bitcast.254, s32[1024]{0:T(1024)S(1)} %broadcast_clamp_fusion), kind=kCustom, calls=%fused_computation.1 | custom fusion | bytes 8392704 | tf_op jit(solution)/shard_map/jit(_take)/gather | solution.py:223
  669.2 5.6 multiply_reduce_fusion
  (333 shorter events, 122.4 us)
Async XLA Ops:
  6.5 8.8 %copy-start.2 = (f32[4,2048]{1,0:T(4,128)S(1)}, f32[4,2048]{1,0:T(4,128)}, u32[]{:S(2)}) copy-start(f32[4,2048]{1,0:T(4,128)} %param.25) | copy-start | bytes 98308
  6.5 8.8 %copy-start.7 = (f32[4]{0:T(128)S(1)}, f32[4]{0:T(128)}, u32[]{:S(2)}) copy-start(f32[4]{0:T(128)} %param.26) | copy-start | bytes 52
  6.5 173.1 %all-gather.2.cloned.1.call-start = ((), (), s32[]{:S(2)}) async-start(), calls=%async_computation.2 | async-start | bytes 17825792 | tf_op jit(solution)/shard_map/all_gather | solution.py:169
  139.5 3.8 copy-start.1
  142.4 12.1 %copy-start.5 = (s32[128,8]{0,1:T(8,128)S(1)}, s32[128,8]{0,1:T(8,128)}, u32[]{:S(2)}) copy-start(s32[128,8]{0,1:T(8,128)} %param.32) | copy-start | bytes 12292
  142.4 12.4 %copy-start.3 = (f32[4096]{0:T(1024)S(1)}, f32[4096]{0:T(1024)}, u32[]{:S(2)}) copy-start(f32[4096]{0:T(1024)} %param.29) | copy-start | bytes 49156
  142.4 21.9 %copy-start.8 = (s32[32]{0:T(128)S(1)}, s32[32]{0:T(128)}, u32[]{:S(2)}) copy-start(s32[32]{0:T(128)} %param.34) | copy-start | bytes 388
  147.9 31.4 %all-to-all-start = ((bf16[16,128,256]{2,1,0:T(8,128)(2,1)}), bf16[16,128,256]{2,1,0:T(8,128)(2,1)S(1)}, u32[]{:S(2)}, u32[]{:S(2)}) async-start(bf16[16,128,256]{2,1,0:T(8,128)(2,1)} %bitcast.11), calls=%async_computation | async-start | bytes 2097152 | tf_op jit(solution)/shard_map/all_to_all | solution.py:164
  191.0 5.4 copy-start
  191.0 5.7 copy-start.4
  215.4 187.2 %all-to-all-start.1 = ((bf16[16,2,64,2048]{3,2,1,0:T(8,128)(2,1)}), bf16[16,2,64,2048]{3,2,1,0:T(8,128)(2,1)}, u32[]{:S(2)}, u32[]{:S(2)}) async-start(bf16[16,2,64,2048]{3,2,1,0:T(8,128)(2,1)} %select_select_fusion), calls=%async_computation.1 | async-start | bytes 16777216 | tf_op jit(solution)/shard_map/all_to_all | solution.py:206
  442.4 8.3 %copy-start.6 = (f32[128,8]{0,1:T(8,128)S(1)}, f32[128,8]{0,1:T(8,128)}, u32[]{:S(2)}) copy-start(f32[128,8]{0,1:T(8,128)} %param.33) | copy-start | bytes 12292
  448.4 13.0 %collective-permute-start = (bf16[1,1,2,64,2048]{4,3,0,2,1:T(8,128)(2,1)}, bf16[1,1,2,64,2048]{4,3,0,2,1:T(8,128)(2,1)}, u32[]{:S(2)}, u32[]{:S(2)}) collective-permute-start(bf16[1,1,2,64,2048]{4,3,0,2,1:T(8,128)(2,1)} %get-tuple-element.208), channel_id=1, source_target_pairs={{0,1},{1,2},{2,3},{3,4},{4,5},{5,6},{6,7},{7,8},{8,9},{9,10},{10,1... | collective-permute-start | bytes 1572872 | tf_op jit(solution)/shard_map/ppermute | solution.py:219
  450.2 22.6 %collective-permute-start.1 = (bf16[1,1,2,64,2048]{4,3,0,2,1:T(8,128)(2,1)}, bf16[1,1,2,64,2048]{4,3,0,2,1:T(8,128)(2,1)}, u32[]{:S(2)}, u32[]{:S(2)}) collective-permute-start(bf16[1,1,2,64,2048]{4,3,0,2,1:T(8,128)(2,1)} %get-tuple-element.207), channel_id=1, source_target_pairs={{0,2},{1,3},{2,4},{3,5},{4,6},{5,7},{6,8},{7,9},{8,10},{9,11},{10,... | collective-permute-start | bytes 1572872 | tf_op jit(solution)/shard_map/ppermute | solution.py:219
  450.3 33.6 %collective-permute-start.2 = (bf16[1,1,2,64,2048]{4,3,0,2,1:T(8,128)(2,1)}, bf16[1,1,2,64,2048]{4,3,0,2,1:T(8,128)(2,1)}, u32[]{:S(2)}, u32[]{:S(2)}) collective-permute-start(bf16[1,1,2,64,2048]{4,3,0,2,1:T(8,128)(2,1)} %get-tuple-element.206), channel_id=1, source_target_pairs={{0,3},{1,4},{2,5},{3,6},{4,7},{5,8},{6,9},{7,10},{8,11},{9,12},{10... | collective-permute-start | bytes 1572872 | tf_op jit(solution)/shard_map/ppermute | solution.py:219
  450.9 94.9 %collective-permute-start.3 = (bf16[1,1,2,64,2048]{4,3,0,2,1:T(8,128)(2,1)}, bf16[1,1,2,64,2048]{4,3,0,2,1:T(8,128)(2,1)S(1)}, u32[]{:S(2)}, u32[]{:S(2)}) collective-permute-start(bf16[1,1,2,64,2048]{4,3,0,2,1:T(8,128)(2,1)} %get-tuple-element.205), channel_id=1, source_target_pairs={{0,4},{1,5},{2,6},{3,7},{4,8},{5,9},{6,10},{7,11},{8,12},{9,13},{1... | collective-permute-start | bytes 1572872 | tf_op jit(solution)/shard_map/ppermute | solution.py:219
  451.8 122.0 %collective-permute-start.4 = (bf16[1,1,2,64,2048]{4,3,0,2,1:T(8,128)(2,1)}, bf16[1,1,2,64,2048]{4,3,0,2,1:T(8,128)(2,1)S(1)}, u32[]{:S(2)}, u32[]{:S(2)}) collective-permute-start(bf16[1,1,2,64,2048]{4,3,0,2,1:T(8,128)(2,1)} %get-tuple-element.204), channel_id=1, source_target_pairs={{0,5},{1,6},{2,7},{3,8},{4,9},{5,10},{6,11},{7,12},{8,13},{9,14},{... | collective-permute-start | bytes 1572872 | tf_op jit(solution)/shard_map/ppermute | solution.py:219
  461.4 129.2 %collective-permute-start.5 = (bf16[1,1,2,64,2048]{4,3,0,2,1:T(8,128)(2,1)}, bf16[1,1,2,64,2048]{4,3,0,2,1:T(8,128)(2,1)S(1)}, u32[]{:S(2)}, u32[]{:S(2)}) collective-permute-start(bf16[1,1,2,64,2048]{4,3,0,2,1:T(8,128)(2,1)} %get-tuple-element.203), channel_id=1, source_target_pairs={{0,6},{1,7},{2,8},{3,9},{4,10},{5,11},{6,12},{7,13},{8,14},{9,15},... | collective-permute-start | bytes 1572872 | tf_op jit(solution)/shard_map/ppermute | solution.py:219
  472.8 134.7 %collective-permute-start.6 = (bf16[1,1,2,64,2048]{4,3,0,2,1:T(8,128)(2,1)}, bf16[1,1,2,64,2048]{4,3,0,2,1:T(8,128)(2,1)S(1)}, u32[]{:S(2)}, u32[]{:S(2)}) collective-permute-start(bf16[1,1,2,64,2048]{4,3,0,2,1:T(8,128)(2,1)} %get-tuple-element.202), channel_id=1, source_target_pairs={{0,7},{1,8},{2,9},{3,10},{4,11},{5,12},{6,13},{7,14},{8,15},{9,0},... | collective-permute-start | bytes 1572872 | tf_op jit(solution)/shard_map/ppermute | solution.py:219
  483.9 140.4 %collective-permute-start.7 = (bf16[1,1,2,64,2048]{4,3,0,2,1:T(8,128)(2,1)}, bf16[1,1,2,64,2048]{4,3,0,2,1:T(8,128)(2,1)S(1)}, u32[]{:S(2)}, u32[]{:S(2)}) collective-permute-start(bf16[1,1,2,64,2048]{4,3,0,2,1:T(8,128)(2,1)} %get-tuple-element.201), channel_id=1, source_target_pairs={{0,8},{1,9},{2,10},{3,11},{4,12},{5,13},{6,14},{7,15},{8,0},{9,1},... | collective-permute-start | bytes 1572872 | tf_op jit(solution)/shard_map/ppermute | solution.py:219
  545.7 79.5 %collective-permute-start.8 = (bf16[1,1,2,64,2048]{4,3,0,2,1:T(8,128)(2,1)}, bf16[1,1,2,64,2048]{4,3,0,2,1:T(8,128)(2,1)S(1)}, u32[]{:S(2)}, u32[]{:S(2)}) collective-permute-start(bf16[1,1,2,64,2048]{4,3,0,2,1:T(8,128)(2,1)} %get-tuple-element.200), channel_id=1, source_target_pairs={{0,9},{1,10},{2,11},{3,12},{4,13},{5,14},{6,15},{7,0},{8,1},{9,2},... | collective-permute-start | bytes 1572872 | tf_op jit(solution)/shard_map/ppermute | solution.py:219
  573.8 52.2 %collective-permute-start.9 = (bf16[1,1,2,64,2048]{4,3,0,2,1:T(8,128)(2,1)}, bf16[1,1,2,64,2048]{4,3,0,2,1:T(8,128)(2,1)S(1)}, u32[]{:S(2)}, u32[]{:S(2)}) collective-permute-start(bf16[1,1,2,64,2048]{4,3,0,2,1:T(8,128)(2,1)} %get-tuple-element.199), channel_id=1, source_target_pairs={{0,10},{1,11},{2,12},{3,13},{4,14},{5,15},{6,0},{7,1},{8,2},{9,3},... | collective-permute-start | bytes 1572872 | tf_op jit(solution)/shard_map/ppermute | solution.py:219
  590.6 36.4 %collective-permute-start.10 = (bf16[1,1,2,64,2048]{4,3,0,2,1:T(8,128)(2,1)}, bf16[1,1,2,64,2048]{4,3,0,2,1:T(8,128)(2,1)S(1)}, u32[]{:S(2)}, u32[]{:S(2)}) collective-permute-start(bf16[1,1,2,64,2048]{4,3,0,2,1:T(8,128)(2,1)} %get-tuple-element.198), channel_id=1, source_target_pairs={{0,11},{1,12},{2,13},{3,14},{4,15},{5,0},{6,1},{7,2},{8,3},{9,4},{... | collective-permute-start | bytes 1572872 | tf_op jit(solution)/shard_map/ppermute | solution.py:219
  607.5 20.4 %collective-permute-start.11 = (bf16[1,1,2,64,2048]{4,3,0,2,1:T(8,128)(2,1)}, bf16[1,1,2,64,2048]{4,3,0,2,1:T(8,128)(2,1)S(1)}, u32[]{:S(2)}, u32[]{:S(2)}) collective-permute-start(bf16[1,1,2,64,2048]{4,3,0,2,1:T(8,128)(2,1)} %get-tuple-element.197), channel_id=1, source_target_pairs={{0,12},{1,13},{2,14},{3,15},{4,0},{5,1},{6,2},{7,3},{8,4},{9,5},{1... | collective-permute-start | bytes 1572872 | tf_op jit(solution)/shard_map/ppermute | solution.py:219
  624.4 10.4 %collective-permute-start.12 = (bf16[1,1,2,64,2048]{4,3,0,2,1:T(8,128)(2,1)S(1)}, bf16[1,1,2,64,2048]{4,3,0,2,1:T(8,128)(2,1)S(1)}, u32[]{:S(2)}, u32[]{:S(2)}) collective-permute-start(bf16[1,1,2,64,2048]{4,3,0,2,1:T(8,128)(2,1)S(1)} %get-tuple-element.196), channel_id=1, source_target_pairs={{0,13},{1,14},{2,15},{3,0},{4,1},{5,2},{6,3},{7,4},{8,5},{9,6},{10... | collective-permute-start | bytes 1572872 | tf_op jit(solution)/shard_map/ppermute | solution.py:219
  625.2 20.8 %collective-permute-start.13 = (bf16[1,1,2,64,2048]{4,3,0,2,1:T(8,128)(2,1)S(1)}, bf16[1,1,2,64,2048]{4,3,0,2,1:T(8,128)(2,1)S(1)}, u32[]{:S(2)}, u32[]{:S(2)}) collective-permute-start(bf16[1,1,2,64,2048]{4,3,0,2,1:T(8,128)(2,1)S(1)} %get-tuple-element.195), channel_id=1, source_target_pairs={{0,14},{1,15},{2,0},{3,1},{4,2},{5,3},{6,4},{7,5},{8,6},{9,7},{10,... | collective-permute-start | bytes 1572872 | tf_op jit(solution)/shard_map/ppermute | solution.py:219
  626.0 20.8 %collective-permute-start.14 = (bf16[1,1,2,64,2048]{4,3,0,2,1:T(8,128)(2,1)S(1)}, bf16[1,1,2,64,2048]{4,3,0,2,1:T(8,128)(2,1)S(1)}, u32[]{:S(2)}, u32[]{:S(2)}) collective-permute-start(bf16[1,1,2,64,2048]{4,3,0,2,1:T(8,128)(2,1)S(1)} %get-tuple-element.194), channel_id=1, source_target_pairs={{0,15},{1,0},{2,1},{3,2},{4,3},{5,4},{6,5},{7,6},{8,7},{9,8},{10,9... | collective-permute-start | bytes 1572872 | tf_op jit(solution)/shard_map/ppermute | solution.py:219
Sparse Core Ops, SparseCore 0:
  9.5 125.3 all-gather.1
